TPU v7x, 32 devices: a whole 2x2x4 slice. The times are simulated.
32 devices in a mesh: group: 2 (over x), trade: 16 (over z, y, core).
Axes of the slice: x: 2, y: 2, z: 4, core: 2. Of those that a mesh axis runs over, the one named last changes fastest.
Arguments:
- factors: bfloat16 [128, 128], P(('group', 'trade')), parts along dimension 0, may hold values from -6 to 6
- loadings: float32 [32, 16], replicated, may hold values from -1.5 to 1.5
- trade_coef: bfloat16 [65536, 256], P(('group', 'trade')), parts along dimension 0, may hold values from -0.75 to 0.75
- basis_size: int32 [65536], P(('group', 'trade')), parts along dimension 0, may hold values from 4 to 32
- set_ids: int32 [65536], P(('group', 'trade')), parts along dimension 0, may hold values from 0 to 31
- live_count: int32 [32], P(('group', 'trade')), parts along dimension 0, may hold values from 1 to 2047, as said below
- netting_row: int32 [64], P('group'), parts along dimension 0, may hold values from 0 to 31, each once
- threshold: float32 [64], P(('group', 'trade')), parts along dimension 0, may hold values from 0.5 to 8
- margin_start: float32 [64, 64], P(('group', 'trade')), parts along dimension 0, may hold values from 0 to 3
Outputs:
- expected: float32 [64, 8], P(('group', 'trade')), parts along dimension 0
There are 2 independent parts, one for each index of `group`. A program takes and returns all parts, laid end to end along the dimension named above; an argument that names none is the same for every part. Nothing has to cross between parts.
Inputs may be any that keep to these rules, and one draw needn't show every extreme that they name: `live_count`: blocks b and b + 8 hold exactly 2048 live trades together.
All inputs are finite; a program needn't handle non-finite values.
Results may differ from a plain program's by a relative error of at most 0.00035.
Values may be sent and summed in bfloat16 or wider, within the bound.
A program may use at most 64 MiB of HBM per device.

v0:
```python
import jax
import jax.numpy as jnp
from jax import lax
from jax.sharding import PartitionSpec as P

F = 16
K = 32
DATES = 8
LAG = 2


def positive_part(netted, margins, limits):
    row_total = netted.shape[0]
    path_count = netted.shape[2]
    margin = jnp.maximum(netted[:, : DATES - LAG] - limits[:, None, None], 0.0)
    held = jnp.broadcast_to(margins[:, None, :], (row_total, LAG, path_count))
    collateral = jnp.concatenate([held, margin], axis=1)
    return jnp.maximum(netted - collateral, 0.0)


def body(
    factors,
    loadings,
    trade_coef,
    basis_size,
    set_ids,
    live_count,
    netting_row,
    threshold,
    margin_start,
):
    part_rows = lax.all_gather(factors, "trade", axis=0, tiled=True)
    row_count = part_rows.shape[0]
    factor_cube = part_rows.astype(jnp.float32).reshape(row_count, DATES, F)
    loaded = jnp.einsum("pdf,kf->pdk", factor_cube, loadings, precision=lax.Precision.HIGHEST)
    basis_table = jnp.tanh(loaded).astype(jnp.bfloat16).reshape(row_count, DATES * K)
    path_total = basis_table.shape[0]
    basis_table = basis_table.reshape(path_total, DATES, K)
    set_total = netting_row.shape[0]
    slot_total = trade_coef.shape[0]
    live_now = live_count[0]
    trade_rows = netting_row[set_ids]
    basis_index = jnp.arange(K, dtype=jnp.int32)
    slot_index = jnp.arange(slot_total, dtype=jnp.int32)
    keep_mask = (basis_index[None, :] < basis_size[:, None]) & (slot_index < live_now)[:, None]
    coef_cube = trade_coef.reshape(slot_total, DATES, K)
    coef_used = jnp.where(keep_mask[:, None, :], coef_cube, jnp.zeros_like(coef_cube))
    slot_now = coef_used.shape[0]
    values = jnp.einsum("tdk,pdk->tdp", coef_used, basis_table, preferred_element_type=jnp.float32)
    values = values.astype(jnp.bfloat16).reshape(slot_now, DATES * path_total)
    set_index = jnp.arange(set_total, dtype=jnp.int32)
    onehot = (trade_rows[None, :] == set_index[:, None]).astype(jnp.bfloat16)
    netted = lax.psum_scatter(
        jnp.dot(onehot, values, preferred_element_type=jnp.float32),
        "trade",
        scatter_dimension=0,
        tiled=True,
    )
    netted = netted.reshape(threshold.shape[0], DATES, path_total)
    shortfall = jnp.sum(positive_part(netted, margin_start, threshold), axis=2)
    return shortfall / path_total


def solution(mesh):
    return jax.shard_map(
        body,
        mesh=mesh,
        in_specs=(
            P(("group", "trade"), None),
            P(),
            P(("group", "trade"), None),
            P(("group", "trade")),
            P(("group", "trade")),
            P(("group", "trade")),
            P("group"),
            P(("group", "trade")),
            P(("group", "trade"), None),
        ),
        out_specs=P(("group", "trade"), None),
        check_vma=False,
    )
```

profile of v0, /device:TPU:0, one launch (start us, length us, event | category | flops | bytes accessed | tf_op | source)
XLA Modules:
  0.0 150.9 jit_solution(146148267404146707)
XLA Ops:
  6.5 0.0 copy-start
  6.5 0.0 copy-start.1
  6.5 0.0 all-reduce.3.cloned.1.call-start
  6.5 1.8 %fusion.14 = (s32[1]{0:T(128)}, s32[1]{0:T(128)}, s32[1]{0:T(128)}, s32[1]{0:T(128)}, s32[1]{0:T(128)}, /*index=5*/s32[1]{0:T(128)}, s32[1]{0:T(128)}, s32[1]{0:...) fusion(s32[32]{0:T(128)} %param.15), kind=kLoop, calls=%fused_computation.25 | loop fusion | bytes 104 | tf_op jit(solution)/shard_map/gather | solution.py:42
  8.4 2.1 %fusion.13 = (s32[1]{0:T(128)}, s32[1]{0:T(128)}, s32[1]{0:T(128)}, s32[1]{0:T(128)}, s32[1]{0:T(128)}, /*index=5*/s32[1]{0:T(128)}, s32[1]{0:T(128)}, s32[1]{0:...) fusion(s32[32]{0:T(128)} %param.15), kind=kLoop, calls=%fused_computation.24 | loop fusion | bytes 152 | tf_op jit(solution)/shard_map/gather | solution.py:42
  10.4 23.4 %all-gather = bf16[16,4,128]{2,1,0:T(4,128)(2,1)S(1)} all-gather(bf16[1,4,128]{2,1,0:T(4,128)(2,1)} %bitcast.47), channel_id=1, replica_groups=mesh['group'=2,'trade'=16] {'trade'}, dimensions={0}, use_global_device_ids=true | all-gather | bytes 17408 | tf_op jit(solution)/shard_map/all_gather | solution.py:32
  33.8 0.1 reshape.48
  34.0 1.5 copy.13
  35.5 0.0 copy-start.2
  36.2 0.0 copy-done
  36.2 0.5 fusion
  36.7 0.0 copy-done.1
  36.7 0.1 fusion.5
  36.7 0.0 copy-start.5
  36.7 0.0 copy-start.4
  36.8 0.0 copy-start.3
  36.8 0.8 convolution_convert_fusion
  37.5 0.0 copy-done.2
  37.5 20.0 %select_select_fusion = s32[2048]{0:T(1024)S(1)} fusion(s32[2048]{0:T(1024)S(1)} %copy-done.2, s32[]{:T(128)} %bitcast, s32[]{:T(128)} %bitcast.1, s32[]{:T(128)} %bitcast.2, s32[]{:T(128)} %bitcast.3, s32[]{:T(128)} %bitcast.4, s32[]{:T(128)} %bitcast.5, s32[]{:T(128)} %bitcast.6, s32[]{:T(128)} %bitcast.7, s32[]{:T(128)} %bitcast.8, s32[]{:T(128)} %bitcast.9, ...), kind=kLoop, calls=%fused_computation.19 | loop fusion | flops 133120 | bytes 16512 | tf_op jit(solution)/shard_map/gather | solution.py:42
  57.6 1.3 fusion.4
  58.9 0.0 all-reduce.3.cloned.1.call-update
  58.9 0.0 copy-done.5
  58.9 0.6 dynamic-slice
  60.2 82.4 %all-reduce.3.cloned.1.call-done = f32[32,512]{1,0:T(8,128)} async-done(((f32[32,512]{1,0:T(8,128)}), f32[32,512]{1,0:T(8,128)}) %all-reduce.3.cloned.1.call-update) | async-done | bytes 65552
  142.5 0.7 constant_dynamic-slice_fusion
  143.2 0.1 reshape.51
  143.3 0.0 copy-done.4
  143.3 0.1 fusion.8
  143.4 0.0 copy-done.3
  143.4 0.1 fusion.10
  143.5 0.6 broadcast_multiply_fusion
  (2 shorter events, 0.0 us)
Async XLA Ops:
  6.5 29.6 %copy-start = (f32[32,16]{0,1:T(8,128)S(1)}, f32[32,16]{0,1:T(8,128)}, u32[]{:S(2)}) copy-start(f32[32,16]{0,1:T(8,128)} %param.10) | copy-start | bytes 6148
  6.5 30.1 %copy-start.1 = (s32[2048]{0:T(1024)S(1)}, s32[2048]{0:T(1024)}, u32[]{:S(2)}) copy-start(s32[2048]{0:T(1024)} %param.12) | copy-start | bytes 24580
  6.5 136.0 %all-reduce.3.cloned.1.call-start = ((), (), s32[]{:S(2)}) async-start(), calls=%async_computation | async-start | bytes 131072
  35.5 2.1 %copy-start.2 = (s32[2048]{0:T(1024)S(1)}, s32[2048]{0:T(1024)}, u32[]{:S(2)}) copy-start(s32[2048]{0:T(1024)} %param.13) | copy-start | bytes 24580
  36.7 22.2 %copy-start.5 = (u32[32]{0:T(128)S(1)}, u32[32]{0:T(128)}, u32[]{:S(2)}) copy-start(u32[32]{0:T(128)} %constant.51) | copy-start | bytes 388
  36.7 106.6 %copy-start.4 = (f32[2]{0:T(128)S(1)}, f32[2]{0:T(128)}, u32[]{:S(2)}) copy-start(f32[2]{0:T(128)} %param.16) | copy-start | bytes 28
  36.8 106.7 %copy-start.3 = (f32[2,64]{1,0:T(2,128)S(1)}, f32[2,64]{1,0:T(2,128)}, u32[]{:S(2)}) copy-start(f32[2,64]{1,0:T(2,128)} %param.17) | copy-start | bytes 1540
Sparse Core Ops, SparseCore 0:
  59.0 83.4 all-reduce.2
where the time goes:
time: 152 us; the launch traced here: 151 us
  waiting for transfers between devices  82.4 us (54%)
  blocking collectives  23.4 us (15%)
  other arithmetic  20.8 us (14%)
  between operations  14.8 us (10%)
  local copies, waits for them, and re-layouts  6.92 us (5%)
  matrix products  2.58 us (2%)
    unnamed x2, waiting for transfers between devices  82.4 us
    all_gather x1, blocking collectives, body(): part_rows = lax.all_gather(factors, 'trade', axis=0, tiled=True)  23.4 us
    gather x1, other arithmetic, body(): trade_rows = netting_row[set_ids]  20 us
    gather x2, local copies, waits for them, and re-layouts, body(): trade_rows = netting_row[set_ids]  3.89 us
  transfers between devices with their start and end apart: 1, of which 1 were waited for; matrix products, arithmetic and copies ran while one was open for 0% of the time, Pallas kernels for 0%

commit v1 on v0

v1 whole, which is shorter than its diff:
```python
import functools

import jax
import jax.numpy as jnp
from jax import lax
from jax.experimental import pallas as pl
from jax.experimental.pallas import tpu as pltpu
from jax.sharding import PartitionSpec as P

F = 16
K = 32
DATES = 8
LAG = 2
LANES = 128
CHUNK = 256
COLS = 512
MESH = pl.DeviceIdType.MESH
f32 = jnp.float32
bf16 = jnp.bfloat16


def iota(shape, axis):
    return lax.broadcasted_iota(jnp.int32, shape, axis)


def kernel(
    n,
    factors,
    loadings,
    trade_coef,
    basis_size,
    set_ids,
    live_count,
    netting_row,
    threshold,
    margin_start,
    out,
    fact,
    load_v,
    coef_v,
    size_v,
    ids_v,
    live_s,
    nrow_v,
    thr_s,
    marg_v,
    split,
    onehot,
    spread,
    basis,
    held,
    acc,
    part,
    recv,
    in_sem,
    gs_sem,
    gr_sem,
    ss_sem,
    sr_sem,
):
    me = lax.axis_index("trade")
    rows = fact.shape[1]
    paths = n * rows
    rep = max(1, LANES // paths)
    width = rep * paths
    slots = coef_v.shape[0]
    owned = recv.shape[1]
    sets = n * owned

    def peer(k):
        return lax.rem(me + k, n)

    def each_peer(step):
        lax.fori_loop(1, n, lambda k, c: (step(peer(k)), c)[1], 0)

    def local(src, dst, i):
        return pltpu.make_async_copy(src, dst, in_sem.at[i])

    barrier = pltpu.get_barrier_semaphore()
    each_peer(lambda j: pl.semaphore_signal(barrier, inc=1, device_id={"trade": j}, device_id_type=MESH))

    copies = [
        local(factors, fact.at[me], 0),
        local(loadings, load_v, 1),
        local(basis_size, size_v, 2),
        local(live_count, live_s, 3),
        local(netting_row, nrow_v, 4),
        local(set_ids, ids_v, 5),
        local(threshold, thr_s, 6),
        local(margin_start, marg_v, 7),
        local(trade_coef, coef_v, 8),
    ]
    for copy in copies:
        copy.start()
    copies[0].wait()
    pl.semaphore_wait(barrier, n - 1)

    def gather(j, slot):
        return pltpu.make_async_remote_copy(
            src_ref=fact.at[me],
            dst_ref=fact.at[me],
            send_sem=gs_sem.at[j],
            recv_sem=gr_sem.at[slot],
            device_id={"trade": j},
            device_id_type=MESH,
        )

    each_peer(lambda j: gather(j, me).start())

    copies[1].wait()
    tiled = (iota((F, LANES), 1) % F == iota((F, LANES), 0)).astype(f32).astype(bf16)
    diag = iota((DATES * K, LANES), 0) // K == iota((DATES * K, LANES), 1) // F
    rest = load_v[...]
    for i in range(3):
        piece = rest.astype(bf16)
        rest = rest - piece.astype(f32)
        wide = jnp.dot(piece, tiled, preferred_element_type=f32)
        wide = jnp.concatenate([wide] * DATES, axis=0)
        split[i] = jnp.where(diag, wide, 0.0).astype(bf16)
    basis[...] = jnp.zeros(basis.shape, bf16)

    copies[4].wait()
    copies[5].wait()
    found = nrow_v[...] == iota((sets, sets), 0)
    owner_set = jnp.sum(jnp.where(found, iota((sets, sets), 1), 0).astype(f32), axis=1, keepdims=True)
    owner_set = owner_set.astype(jnp.int32)
    for c in range(slots // CHUNK):
        cut = slice(c * CHUNK, (c + 1) * CHUNK)
        onehot[:, cut] = (ids_v[:, cut] == owner_set).astype(f32).astype(bf16)

    copies[7].wait()
    for i in range(LAG):
        held[:, i * paths : (i + 1) * paths] = marg_v[...]

    for i in (2, 3, 8):
        copies[i].wait()
    live_now = live_s[0]
    slot_index = iota(size_v.shape, 0) * LANES + iota(size_v.shape, 1)
    used = jnp.where(slot_index < live_now, size_v[...], 0).astype(f32)
    basis_index = (iota((LANES, LANES), 1) % K).astype(f32)
    for c in range(slots // LANES):
        limit = jnp.broadcast_to(used[c : c + 1], (LANES, LANES)).T
        keep = basis_index < limit
        cut = slice(c * LANES, (c + 1) * LANES)
        for h in range(0, DATES * K, LANES):
            side = slice(h, h + LANES)
            coef_v[cut, side] = jnp.where(keep, coef_v[cut, side].astype(f32), 0.0).astype(bf16)
    copies[6].wait()

    each_peer(lambda j: gather(j, j).wait_recv())

    for j in range(n):
        block = fact[j].astype(f32)
        for i in range(rep):
            at = i * paths + j * rows
            spread[at : at + rows] = block
    table = spread[...].astype(bf16)
    dims = (((1,), (1,)), ((), ()))
    loaded = lax.dot_general(split[2], table, dims, preferred_element_type=f32)
    loaded += lax.dot_general(split[1], table, dims, preferred_element_type=f32)
    loaded += lax.dot_general(split[0], table, dims, preferred_element_type=f32)
    bent = jnp.tanh(loaded)
    tall = rep * K
    pair = iota((tall, width), 0) // K == iota((tall, width), 1) // paths
    for j in range(DATES // rep):
        strip = jnp.where(pair, bent[j * tall : (j + 1) * tall], 0.0).astype(bf16)
        basis[j * tall : (j + 1) * tall, j * width : (j + 1) * width] = strip

    def block_sums(right):
        total = None
        for c in range(slots // CHUNK):
            cut = slice(c * CHUNK, (c + 1) * CHUNK)
            values = jnp.dot(coef_v[cut], right, preferred_element_type=f32).astype(bf16)
            term = jnp.dot(onehot[:, cut], values, preferred_element_type=f32)
            total = term if total is None else total + term
        return total

    blocks = acc.shape[1] // COLS
    if blocks == 1:
        acc[...] = block_sums(basis[...])
    else:

        def one(b, carry):
            side = pl.ds(pl.multiple_of(b * COLS, COLS), COLS)
            acc[:, side] = block_sums(basis[:, side])
            return carry

        lax.fori_loop(0, blocks, one, 0)
    for j in range(n):
        part[j] = acc[j * owned : (j + 1) * owned]

    def scatter(j, slot):
        return pltpu.make_async_remote_copy(
            src_ref=part.at[j],
            dst_ref=recv.at[me],
            send_sem=ss_sem.at[j],
            recv_sem=sr_sem.at[slot],
            device_id={"trade": j},
            device_id_type=MESH,
        )

    each_peer(lambda j: scatter(j, me).start())
    recv[me] = part[me]
    each_peer(lambda j: scatter(j, j).wait_recv())

    netted = recv[0]
    for j in range(1, n):
        netted = netted + recv[j]
    row_at = iota((owned, 1), 0)
    limits = jnp.zeros((owned, 1), f32)
    for r in range(owned):
        limits = jnp.where(row_at == r, thr_s[r], limits)
    first = LAG * paths
    margin = jnp.maximum(netted[:, : (DATES - LAG) * paths] - limits, 0.0)
    head = jnp.maximum(netted[:, :first] - held[...], 0.0)
    tail = jnp.maximum(netted[:, first:] - margin, 0.0)
    result = jnp.zeros(out.shape, f32)
    lane_date = iota((owned, width), 1) // paths
    column = iota(out.shape, 1)
    for j in range(DATES // rep):
        at = j * width
        block = head[:, at : at + width] if at < first else tail[:, at - first : at - first + width]
        for i in range(rep):
            own = jnp.where(lane_date == i, block, 0.0) if rep > 1 else block
            result = jnp.where(column == j * rep + i, jnp.sum(own, axis=1, keepdims=True), result)
    out[...] = result
    each_peer(lambda j: gather(j, j).wait_send())
    each_peer(lambda j: scatter(j, j).wait_send())


def body(n, factors, loadings, trade_coef, basis_size, set_ids, live_count, netting_row, threshold, margin_start):
    rows = factors.shape[0]
    paths = n * rows
    rep = max(1, LANES // paths)
    slots = trade_coef.shape[0]
    sets = netting_row.shape[0]
    owned = threshold.shape[0]
    wide = DATES * paths
    hbm = pl.BlockSpec(memory_space=pltpu.MemorySpace.HBM)
    total = pl.pallas_call(
        functools.partial(kernel, n),
        out_shape=jax.ShapeDtypeStruct((owned, DATES), f32),
        in_specs=[hbm] * 9,
        out_specs=pl.BlockSpec(memory_space=pltpu.VMEM),
        scratch_shapes=[
            pltpu.VMEM((n, rows, DATES * F), bf16),
            pltpu.VMEM((K, F), f32),
            pltpu.VMEM((slots, DATES * K), bf16),
            pltpu.VMEM((slots // LANES, LANES), jnp.int32),
            pltpu.VMEM((1, slots), jnp.int32),
            pltpu.SMEM((1,), jnp.int32),
            pltpu.VMEM((1, sets), jnp.int32),
            pltpu.SMEM((owned,), f32),
            pltpu.VMEM((owned, paths), f32),
            pltpu.VMEM((3, DATES * K, DATES * F), bf16),
            pltpu.VMEM((sets, slots), bf16),
            pltpu.VMEM((rep * paths, DATES * F), f32),
            pltpu.VMEM((DATES * K, wide), bf16),
            pltpu.VMEM((owned, LAG * paths), f32),
            pltpu.VMEM((sets, wide), f32),
            pltpu.VMEM((n, owned, wide), f32),
            pltpu.VMEM((n, owned, wide), f32),
            pltpu.SemaphoreType.DMA((9,)),
            pltpu.SemaphoreType.DMA((n,)),
            pltpu.SemaphoreType.DMA((n,)),
            pltpu.SemaphoreType.DMA((n,)),
            pltpu.SemaphoreType.DMA((n,)),
        ],
        compiler_params=pltpu.CompilerParams(
            collective_id=0, has_side_effects=True, vmem_limit_bytes=48 * 2**20
        ),
    )(
        factors,
        loadings,
        trade_coef,
        basis_size.reshape(slots // LANES, LANES),
        set_ids.reshape(1, slots),
        live_count,
        netting_row.reshape(1, sets),
        threshold,
        margin_start,
    )
    return total / paths


def solution(mesh):
    return jax.shard_map(
        functools.partial(body, mesh.shape["trade"]),
        mesh=mesh,
        in_specs=(
            P(("group", "trade"), None),
            P(),
            P(("group", "trade"), None),
            P(("group", "trade")),
            P(("group", "trade")),
            P(("group", "trade")),
            P("group"),
            P(("group", "trade")),
            P(("group", "trade"), None),
        ),
        out_specs=P(("group", "trade"), None),
        check_vma=False,
    )
```

time: 152 us -> 20.3 us (0.13)
  waiting for transfers between devices: 82.4 us -> 0 us
  blocking collectives: 23.4 us -> 0 us
  other arithmetic: 20.8 us -> 0.56 us
  Pallas kernels: 0 us -> 16.7 us
  between operations: 14.8 us -> 0.75 us
  local copies, waits for them, and re-layouts: 6.92 us -> 2.05 us
  matrix products: 2.58 us -> 0 us
    unnamed x2 -> x0, waiting for transfers between devices: 82.4 us -> none
    all_gather x1 -> x0, blocking collectives: 23.4 us -> none  [body(): part_rows = lax.all_gather(factors, 'trade', axis=0, tiled=True)]
    gather x1 -> x0, other arithmetic: 20 us -> none  [body(): trade_rows = netting_row[set_ids]]
    pallas_call x0 -> x1, Pallas kernels: none -> 16.7 us  [body(): pl.pallas_call(functools.partial(kernel, n), out_shape=jax.ShapeDtypeStru...]
    gather x2 -> x0, local copies, waits for them, and re-layouts: 3.89 us -> none  [body(): trade_rows = netting_row[set_ids]]
    dot_general x3 -> x0, matrix products: 2.58 us -> none  [the longest x1 1.33 us: body(): jnp.dot(onehot, values, preferred_element_type=jnp.float32)]
  transfers between devices with their start and end apart: 1 -> 0, of which waited for: 1 -> 0; matrix products, arithmetic and copies ran while one was open for 0% -> 0% of each run, Pallas kernels for 0% -> 0%
where the time goes in v1:
time: 20.3 us; the launch traced here: 20.1 us
  Pallas kernels  16.7 us (82%)
  local copies, waits for them, and re-layouts  2.05 us (10%)
  between operations  0.75 us (4%)
  other arithmetic  0.56 us (3%)
    pallas_call x1, Pallas kernels, body(): pl.pallas_call(functools.partial(kernel, n), out_shape=jax.ShapeDtypeStru...  16.7 us
    unnamed x15, local copies, waits for them, and re-layouts  2.05 us
    div x1, other arithmetic, body(): return total / paths  0.56 us

profile of v1, /device:TPU:0, one launch (start us, length us, event | category | flops | bytes accessed | tf_op | source)
XLA Modules:
  0.0 20.1 jit_solution(3386174090481486573)
XLA Ops:
  0.7 0.0 copy-start.1
  0.7 0.0 copy-start.2
  0.7 0.0 copy-start.3
  0.7 0.0 copy-start.4
  0.7 0.0 copy-start.5
  0.7 0.0 copy-start.6
  0.7 0.8 %copy.10.loadings = f32[32,16]{1,0:T(8,128)S(1)} copy(f32[32,16]{0,1:T(8,128)} %param.10) | data formatting | bytes 4096 | tf_op args[1]
  1.5 0.0 copy-done.1
  1.5 0.0 copy-done.2
  1.5 0.0 copy-done.3
  1.5 0.0 copy-done.4
  1.5 0.0 copy-done.5
  1.6 0.0 copy-done.6
  1.6 0.0 copy-start
  1.6 1.2 %copy-done = bf16[2048,256]{1,0:T(8,128)(2,1)S(1)} copy-done((bf16[2048,256]{1,0:T(8,128)(2,1)S(1)}, bf16[2048,256]{1,0:T(8,128)(2,1)}, u32[]{:S(2)}) %copy-start) | copy-done | bytes 1048600
  2.8 16.7 %shard_map.91 = f32[2,8]{1,0:T(2,128)S(1)} custom-call(bf16[4,128]{1,0:T(4,128)(2,1)S(1)} %copy-done.3, f32[32,16]{1,0:T(8,128)S(1)} %copy.10.loadings, bf16[2048,256]{1,0:T(8,128)(2,1)S(1)} %copy-done, s32[16,128]{1,0:T(8,128)S(1)} %bitcast.3, s32[1,2048]{1,0:T(1,128)S(1)} %bitcast.4, s32[1]{0:T(128)S(6)} %copy.11.live_count, s32[1,32]{1,0:T(1,128)S(1)} %bitcast.5, ...), custom_call_target="tpu_custom_call" | custom-call | tf_op jit(solution)/shard_map/pallas_call | solution.py:240
  19.5 0.6 %broadcast_multiply_fusion = f32[2,8]{1,0:T(2,128)} fusion(f32[2,8]{1,0:T(2,128)S(1)} %shard_map.91), kind=kLoop, calls=%fused_computation | loop fusion | flops 16 | bytes 128 | tf_op jit(solution)/shard_map/div | solution.py:283
Async XLA Ops:
  0.7 0.9 %copy-start.1 = (s32[2048]{0:T(1024)S(1)}, s32[2048]{0:T(1024)}, u32[]{:S(2)}) copy-start(s32[2048]{0:T(1024)} %param.12) | copy-start | bytes 24580
  0.7 0.9 %copy-start.2 = (s32[2048]{0:T(1024)S(1)}, s32[2048]{0:T(1024)}, u32[]{:S(2)}) copy-start(s32[2048]{0:T(1024)} %param.13) | copy-start | bytes 24580
  0.7 0.9 %copy-start.3 = (bf16[4,128]{1,0:T(4,128)(2,1)S(1)}, bf16[4,128]{1,0:T(4,128)(2,1)}, u32[]{:S(2)}) copy-start(bf16[4,128]{1,0:T(4,128)(2,1)} %factors.1) | copy-start | bytes 3076
  0.7 0.9 %copy-start.4 = (f32[2,64]{1,0:T(2,128)S(1)}, f32[2,64]{1,0:T(2,128)}, u32[]{:S(2)}) copy-start(f32[2,64]{1,0:T(2,128)} %margin_start.1) | copy-start | bytes 1540
  0.7 0.9 %copy-start.5 = (s32[32]{0:T(128)S(1)}, s32[32]{0:T(128)}, u32[]{:S(2)}) copy-start(s32[32]{0:T(128)} %param.15) | copy-start | bytes 388
  0.7 0.9 %copy-start.6 = (f32[2]{0:T(128)S(1)}, f32[2]{0:T(128)}, u32[]{:S(2)}) copy-start(f32[2]{0:T(128)} %threshold.1) | copy-start | bytes 28
  1.6 1.2 %copy-start = (bf16[2048,256]{1,0:T(8,128)(2,1)S(1)}, bf16[2048,256]{1,0:T(8,128)(2,1)}, u32[]{:S(2)}) copy-start(bf16[2048,256]{1,0:T(8,128)(2,1)} %trade_coef.1) | copy-start | bytes 3145732

commit v2 on v1

--- a/solution.py
+++ b/solution.py
@@ -40,7 +40,6 @@
     coef_v,
     size_v,
     ids_v,
-    live_s,
     nrow_v,
     thr_s,
     marg_v,
@@ -83,12 +82,11 @@
         local(factors, fact.at[me], 0),
         local(loadings, load_v, 1),
         local(basis_size, size_v, 2),
-        local(live_count, live_s, 3),
+        local(threshold, thr_s, 3),
         local(netting_row, nrow_v, 4),
         local(set_ids, ids_v, 5),
-        local(threshold, thr_s, 6),
-        local(margin_start, marg_v, 7),
-        local(trade_coef, coef_v, 8),
+        local(margin_start, marg_v, 6),
+        local(trade_coef, coef_v, 7),
     ]
     for copy in copies:
         copy.start()
@@ -114,7 +112,7 @@
     for i in range(3):
         piece = rest.astype(bf16)
         rest = rest - piece.astype(f32)
-        wide = jnp.dot(piece, tiled, preferred_element_type=f32)
+        wide = lax.dot_general(piece, tiled, (((0,), (0,)), ((), ())), preferred_element_type=f32)
         wide = jnp.concatenate([wide] * DATES, axis=0)
         split[i] = jnp.where(diag, wide, 0.0).astype(bf16)
     basis[...] = jnp.zeros(basis.shape, bf16)
@@ -128,13 +126,13 @@
         cut = slice(c * CHUNK, (c + 1) * CHUNK)
         onehot[:, cut] = (ids_v[:, cut] == owner_set).astype(f32).astype(bf16)
 
-    copies[7].wait()
+    copies[6].wait()
     for i in range(LAG):
         held[:, i * paths : (i + 1) * paths] = marg_v[...]
 
-    for i in (2, 3, 8):
+    for i in (2, 3, 7):
         copies[i].wait()
-    live_now = live_s[0]
+    live_now = live_count[0]
     slot_index = iota(size_v.shape, 0) * LANES + iota(size_v.shape, 1)
     used = jnp.where(slot_index < live_now, size_v[...], 0).astype(f32)
     basis_index = (iota((LANES, LANES), 1) % K).astype(f32)
@@ -145,7 +143,6 @@
         for h in range(0, DATES * K, LANES):
             side = slice(h, h + LANES)
             coef_v[cut, side] = jnp.where(keep, coef_v[cut, side].astype(f32), 0.0).astype(bf16)
-    copies[6].wait()
 
     each_peer(lambda j: gather(j, j).wait_recv())
 
@@ -240,15 +237,14 @@
     total = pl.pallas_call(
         functools.partial(kernel, n),
         out_shape=jax.ShapeDtypeStruct((owned, DATES), f32),
-        in_specs=[hbm] * 9,
+        in_specs=[hbm] * 5 + [pl.BlockSpec(memory_space=pltpu.SMEM)] + [hbm] * 3,
         out_specs=pl.BlockSpec(memory_space=pltpu.VMEM),
         scratch_shapes=[
             pltpu.VMEM((n, rows, DATES * F), bf16),
-            pltpu.VMEM((K, F), f32),
+            pltpu.VMEM((F, K), f32),
             pltpu.VMEM((slots, DATES * K), bf16),
             pltpu.VMEM((slots // LANES, LANES), jnp.int32),
             pltpu.VMEM((1, slots), jnp.int32),
-            pltpu.SMEM((1,), jnp.int32),
             pltpu.VMEM((1, sets), jnp.int32),
             pltpu.SMEM((owned,), f32),
             pltpu.VMEM((owned, paths), f32),
@@ -260,18 +256,18 @@
             pltpu.VMEM((sets, wide), f32),
             pltpu.VMEM((n, owned, wide), f32),
             pltpu.VMEM((n, owned, wide), f32),
-            pltpu.SemaphoreType.DMA((9,)),
+            pltpu.SemaphoreType.DMA((8,)),
             pltpu.SemaphoreType.DMA((n,)),
             pltpu.SemaphoreType.DMA((n,)),
             pltpu.SemaphoreType.DMA((n,)),
             pltpu.SemaphoreType.DMA((n,)),
         ],
         compiler_params=pltpu.CompilerParams(
-            collective_id=0, has_side_effects=True, vmem_limit_bytes=48 * 2**20
+            collective_id=0, has_side_effects=True, vmem_limit_bytes=67043328
         ),
     )(
         factors,
-        loadings,
+        loadings.T,
         trade_coef,
         basis_size.reshape(slots // LANES, LANES),
         set_ids.reshape(1, slots),

time: 20.3 us -> 19.4 us (0.956)
  local copies, waits for them, and re-layouts: 2.05 us -> 0 us
  Pallas kernels: 16.7 us -> 17.4 us
  other arithmetic: 0.56 us -> 1.24 us
    unnamed x15 -> x0, local copies, waits for them, and re-layouts: 2.05 us -> none
    div x1, other arithmetic: 0.56 us -> 1.24 us  [body(): return total / paths]
    pallas_call x1, Pallas kernels: 16.7 us -> 17.4 us  [body(): pl.pallas_call(functools.partial(kernel, n), out_shape=jax.ShapeDtypeStru...]
where the time goes in v2:
time: 19.4 us; the launch traced here: 19.3 us
  Pallas kernels  17.4 us (90%)
  other arithmetic  1.24 us (6%)
  between operations  0.66 us (3%)
    pallas_call x1, Pallas kernels, body(): pl.pallas_call(functools.partial(kernel, n), out_shape=jax.ShapeDtypeStru...  17.4 us
    div x1, other arithmetic, body(): return total / paths  1.24 us

profile of v2, /device:TPU:0, one launch (start us, length us, event | category | flops | bytes accessed | tf_op | source)
XLA Modules:
  0.0 19.3 jit_solution(13653028844085207468)
XLA Ops:
  0.7 17.4 %shard_map.91 = f32[2,8]{1,0:T(2,128)} custom-call(bf16[4,128]{1,0:T(4,128)(2,1)} %factors.1, f32[16,32]{1,0:T(8,128)} %bitcast.4, bf16[2048,256]{1,0:T(8,128)(2,1)} %trade_coef.1, s32[16,128]{1,0:T(8,128)} %bitcast.5, s32[1,2048]{1,0:T(1,128)} %bitcast.6, s32[1]{0:T(128)S(6)} %copy.10.live_count, s32[1,32]{1,0:T(1,128)} %bitcast.7, f32[2]{0:T(128)} %threshold.1, ...), custom_call_target="tpu_custom_call" | custom-call | tf_op jit(solution)/shard_map/pallas_call | solution.py:237
  18.0 1.2 %broadcast_multiply_fusion = f32[2,8]{1,0:T(2,128)} fusion(f32[2,8]{1,0:T(2,128)} %shard_map.91), kind=kLoop, calls=%fused_computation | loop fusion | flops 16 | bytes 128 | tf_op jit(solution)/shard_map/div | solution.py:279

commit v3 on v2

--- a/solution.py
+++ b/solution.py
@@ -225,6 +225,10 @@
     each_peer(lambda j: scatter(j, j).wait_send())
 
 
+def stay(x):
+    return pltpu.with_memory_space_constraint(x, pltpu.MemorySpace.HBM)
+
+
 def body(n, factors, loadings, trade_coef, basis_size, set_ids, live_count, netting_row, threshold, margin_start):
     rows = factors.shape[0]
     paths = n * rows
@@ -263,18 +267,18 @@
             pltpu.SemaphoreType.DMA((n,)),
         ],
         compiler_params=pltpu.CompilerParams(
-            collective_id=0, has_side_effects=True, vmem_limit_bytes=67043328
+            collective_id=0, has_side_effects=True, vmem_limit_bytes=48 * 2**20
         ),
     )(
-        factors,
-        loadings.T,
-        trade_coef,
-        basis_size.reshape(slots // LANES, LANES),
-        set_ids.reshape(1, slots),
+        stay(factors),
+        stay(loadings.T),
+        stay(trade_coef),
+        stay(basis_size.reshape(slots // LANES, LANES)),
+        stay(set_ids.reshape(1, slots)),
         live_count,
-        netting_row.reshape(1, sets),
-        threshold,
-        margin_start,
+        stay(netting_row.reshape(1, sets)),
+        stay(threshold),
+        stay(margin_start),
     )
     return total / paths
 

time: 19.4 us -> 18.2 us (0.938)
  other arithmetic: 1.24 us -> 0.56 us
  Pallas kernels: 17.4 us -> 16.8 us
    div x1, other arithmetic: 1.24 us -> 0.56 us  [body(): return total / paths]
    pallas_call x1, Pallas kernels: 17.4 us -> 16.8 us  [body(): pl.pallas_call(functools.partial(kernel, n), out_shape=jax.ShapeDtypeStru...]
where the time goes in v3:
time: 18.2 us; the launch traced here: 18 us
  Pallas kernels  16.8 us (92%)
  between operations  0.66 us (4%)
  other arithmetic  0.56 us (3%)
    pallas_call x1, Pallas kernels, body(): pl.pallas_call(functools.partial(kernel, n), out_shape=jax.ShapeDtypeStru...  16.8 us
    div x1, other arithmetic, body(): return total / paths  0.56 us

profile of v3, /device:TPU:0, one launch (start us, length us, event | category | flops | bytes accessed | tf_op | source)
XLA Modules:
  0.0 18.0 jit_solution(11421392996042319851)
XLA Ops:
  0.7 16.8 %shard_map.91 = f32[2,8]{1,0:T(2,128)S(1)} custom-call(bf16[4,128]{1,0:T(4,128)(2,1)} %factors.1, f32[16,32]{1,0:T(8,128)} %bitcast.4, bf16[2048,256]{1,0:T(8,128)(2,1)} %trade_coef.1, s32[16,128]{1,0:T(8,128)} %bitcast.5, s32[1,2048]{1,0:T(1,128)} %bitcast.6, s32[1]{0:T(128)S(6)} %copy.10.live_count, s32[1,32]{1,0:T(1,128)} %bitcast.7, f32[2]{0:T(128)} %threshold.1, ...), custom_call_target="tpu_custom_call" | custom-call | tf_op jit(solution)/shard_map/pallas_call | solution.py:241
  17.4 0.6 %broadcast_multiply_fusion = f32[2,8]{1,0:T(2,128)} fusion(f32[2,8]{1,0:T(2,128)S(1)} %shard_map.91), kind=kLoop, calls=%fused_computation | loop fusion | flops 16 | bytes 128 | tf_op jit(solution)/shard_map/div | solution.py:283

commit v4 on v3

--- a/solution.py
+++ b/solution.py
@@ -75,37 +75,44 @@
     def local(src, dst, i):
         return pltpu.make_async_copy(src, dst, in_sem.at[i])
 
+    def settle(ref, sem):
+        rest = ref.at[pl.ds(0, n - 1)]
+        pltpu.make_async_copy(rest, rest, sem).wait()
+
     barrier = pltpu.get_barrier_semaphore()
     each_peer(lambda j: pl.semaphore_signal(barrier, inc=1, device_id={"trade": j}, device_id_type=MESH))
 
-    copies = [
-        local(factors, fact.at[me], 0),
-        local(loadings, load_v, 1),
-        local(basis_size, size_v, 2),
-        local(threshold, thr_s, 3),
-        local(netting_row, nrow_v, 4),
-        local(set_ids, ids_v, 5),
-        local(margin_start, marg_v, 6),
-        local(trade_coef, coef_v, 7),
-    ]
-    for copy in copies:
+    own = local(factors, fact.at[me], 0)
+    limit_copy = local(threshold, thr_s, 1)
+    pairs = (
+        (loadings, load_v),
+        (basis_size, size_v),
+        (netting_row, nrow_v),
+        (set_ids, ids_v),
+        (margin_start, marg_v),
+        (trade_coef, coef_v),
+    )
+    copies = [local(src, dst, 2) for src, dst in pairs]
+    for copy in (own, *copies, limit_copy):
         copy.start()
-    copies[0].wait()
+    own.wait()
     pl.semaphore_wait(barrier, n - 1)
 
-    def gather(j, slot):
+    def gather(j):
         return pltpu.make_async_remote_copy(
             src_ref=fact.at[me],
             dst_ref=fact.at[me],
-            send_sem=gs_sem.at[j],
-            recv_sem=gr_sem.at[slot],
+            send_sem=gs_sem,
+            recv_sem=gr_sem,
             device_id={"trade": j},
             device_id_type=MESH,
         )
 
-    each_peer(lambda j: gather(j, me).start())
-
-    copies[1].wait()
+    each_peer(lambda j: gather(j).start())
+
+    for copy in copies:
+        copy.wait()
+    limit_copy.wait()
     tiled = (iota((F, LANES), 1) % F == iota((F, LANES), 0)).astype(f32).astype(bf16)
     diag = iota((DATES * K, LANES), 0) // K == iota((DATES * K, LANES), 1) // F
     rest = load_v[...]
@@ -117,8 +124,6 @@
         split[i] = jnp.where(diag, wide, 0.0).astype(bf16)
     basis[...] = jnp.zeros(basis.shape, bf16)
 
-    copies[4].wait()
-    copies[5].wait()
     found = nrow_v[...] == iota((sets, sets), 0)
     owner_set = jnp.sum(jnp.where(found, iota((sets, sets), 1), 0).astype(f32), axis=1, keepdims=True)
     owner_set = owner_set.astype(jnp.int32)
@@ -126,12 +131,9 @@
         cut = slice(c * CHUNK, (c + 1) * CHUNK)
         onehot[:, cut] = (ids_v[:, cut] == owner_set).astype(f32).astype(bf16)
 
-    copies[6].wait()
     for i in range(LAG):
         held[:, i * paths : (i + 1) * paths] = marg_v[...]
 
-    for i in (2, 3, 7):
-        copies[i].wait()
     live_now = live_count[0]
     slot_index = iota(size_v.shape, 0) * LANES + iota(size_v.shape, 1)
     used = jnp.where(slot_index < live_now, size_v[...], 0).astype(f32)
@@ -144,7 +146,7 @@
             side = slice(h, h + LANES)
             coef_v[cut, side] = jnp.where(keep, coef_v[cut, side].astype(f32), 0.0).astype(bf16)
 
-    each_peer(lambda j: gather(j, j).wait_recv())
+    settle(fact, gr_sem)
 
     for j in range(n):
         block = fact[j].astype(f32)
@@ -186,19 +188,19 @@
     for j in range(n):
         part[j] = acc[j * owned : (j + 1) * owned]
 
-    def scatter(j, slot):
+    def scatter(j):
         return pltpu.make_async_remote_copy(
             src_ref=part.at[j],
             dst_ref=recv.at[me],
-            send_sem=ss_sem.at[j],
-            recv_sem=sr_sem.at[slot],
+            send_sem=ss_sem,
+            recv_sem=sr_sem,
             device_id={"trade": j},
             device_id_type=MESH,
         )
 
-    each_peer(lambda j: scatter(j, me).start())
+    each_peer(lambda j: scatter(j).start())
     recv[me] = part[me]
-    each_peer(lambda j: scatter(j, j).wait_recv())
+    settle(recv, sr_sem)
 
     netted = recv[0]
     for j in range(1, n):
@@ -221,8 +223,8 @@
             own = jnp.where(lane_date == i, block, 0.0) if rep > 1 else block
             result = jnp.where(column == j * rep + i, jnp.sum(own, axis=1, keepdims=True), result)
     out[...] = result
-    each_peer(lambda j: gather(j, j).wait_send())
-    each_peer(lambda j: scatter(j, j).wait_send())
+    settle(fact, gs_sem)
+    settle(recv, ss_sem)
 
 
 def stay(x):
@@ -260,11 +262,11 @@
             pltpu.VMEM((sets, wide), f32),
             pltpu.VMEM((n, owned, wide), f32),
             pltpu.VMEM((n, owned, wide), f32),
-            pltpu.SemaphoreType.DMA((8,)),
-            pltpu.SemaphoreType.DMA((n,)),
-            pltpu.SemaphoreType.DMA((n,)),
-            pltpu.SemaphoreType.DMA((n,)),
-            pltpu.SemaphoreType.DMA((n,)),
+            pltpu.SemaphoreType.DMA((3,)),
+            pltpu.SemaphoreType.DMA,
+            pltpu.SemaphoreType.DMA,
+            pltpu.SemaphoreType.DMA,
+            pltpu.SemaphoreType.DMA,
         ],
         compiler_params=pltpu.CompilerParams(
             collective_id=0, has_side_effects=True, vmem_limit_bytes=48 * 2**20

time: 18.2 us -> 17.3 us (0.951)
  Pallas kernels: 16.8 us -> 15.9 us
    pallas_call x1, Pallas kernels: 16.8 us -> 15.9 us  [body(): pl.pallas_call(functools.partial(kernel, n), out_shape=jax.ShapeDtypeStru...]
where the time goes in v4:
time: 17.3 us; the launch traced here: 17.1 us
  Pallas kernels  15.9 us (92%)
  between operations  0.66 us (4%)
  other arithmetic  0.56 us (3%)
    pallas_call x1, Pallas kernels, body(): pl.pallas_call(functools.partial(kernel, n), out_shape=jax.ShapeDtypeStru...  15.9 us
    div x1, other arithmetic, body(): return total / paths  0.56 us

profile of v4, /device:TPU:0, one launch (start us, length us, event | category | flops | bytes accessed | tf_op | source)
XLA Modules:
  0.0 17.1 jit_solution(3970042138407458737)
XLA Ops:
  0.7 15.9 %shard_map.91 = f32[2,8]{1,0:T(2,128)S(1)} custom-call(bf16[4,128]{1,0:T(4,128)(2,1)} %factors.1, f32[16,32]{1,0:T(8,128)} %bitcast.4, bf16[2048,256]{1,0:T(8,128)(2,1)} %trade_coef.1, s32[16,128]{1,0:T(8,128)} %bitcast.5, s32[1,2048]{1,0:T(1,128)} %bitcast.6, s32[1]{0:T(128)S(6)} %copy.10.live_count, s32[1,32]{1,0:T(1,128)} %bitcast.7, f32[2]{0:T(128)} %threshold.1, ...), custom_call_target="tpu_custom_call" | custom-call | tf_op jit(solution)/shard_map/pallas_call | solution.py:243
  16.5 0.6 %broadcast_multiply_fusion = f32[2,8]{1,0:T(2,128)} fusion(f32[2,8]{1,0:T(2,128)S(1)} %shard_map.91), kind=kLoop, calls=%fused_computation | loop fusion | flops 16 | bytes 128 | tf_op jit(solution)/shard_map/div | solution.py:285

commit v5 on v4

--- a/solution.py
+++ b/solution.py
@@ -21,6 +21,10 @@
 
 def iota(shape, axis):
     return lax.broadcasted_iota(jnp.int32, shape, axis)
+
+
+def plane_size(n):
+    return 1 << ((n.bit_length() - 1) // 2)
 
 
 def kernel(
@@ -53,7 +57,11 @@
     recv,
     in_sem,
     gs_sem,
-    gr_sem,
+    up_sem,
+    near_sem,
+    high_sem,
+    low_sem,
+    ready,
     ss_sem,
     sr_sem,
 ):
@@ -69,18 +77,36 @@
     def peer(k):
         return lax.rem(me + k, n)
 
+    plane = plane_size(n)
+    levels = n // plane
+    level = lax.div(me, plane)
+    spot = lax.rem(me, plane)
+    inner = level < levels - 1
+
+    def each_of(low, high, step):
+        lax.fori_loop(low, high, lambda j, c: (step(j), c)[1], 0)
+
+    def each_near(step):
+        for k in range(1, plane):
+            step(level * plane + lax.rem(spot + k, plane))
+
     def each_peer(step):
         lax.fori_loop(1, n, lambda k, c: (step(peer(k)), c)[1], 0)
 
     def local(src, dst, i):
         return pltpu.make_async_copy(src, dst, in_sem.at[i])
 
-    def settle(ref, sem):
-        rest = ref.at[pl.ds(0, n - 1)]
+    def settle(ref, sem, count):
+        rest = ref.at[pl.ds(0, count)]
         pltpu.make_async_copy(rest, rest, sem).wait()
 
     barrier = pltpu.get_barrier_semaphore()
-    each_peer(lambda j: pl.semaphore_signal(barrier, inc=1, device_id={"trade": j}, device_id_type=MESH))
+
+    def greet(j):
+        pl.semaphore_signal(barrier, inc=1, device_id={"trade": j}, device_id_type=MESH)
+
+    each_near(greet)
+    each_of((level + 1) * plane, n, greet)
 
     own = local(factors, fact.at[me], 0)
     limit_copy = local(threshold, thr_s, 1)
@@ -95,20 +121,25 @@
     copies = [local(src, dst, 2) for src, dst in pairs]
     for copy in (own, *copies, limit_copy):
         copy.start()
-    own.wait()
-    pl.semaphore_wait(barrier, n - 1)
-
-    def gather(j):
-        return pltpu.make_async_remote_copy(
-            src_ref=fact.at[me],
-            dst_ref=fact.at[me],
-            send_sem=gs_sem,
-            recv_sem=gr_sem,
+    pl.semaphore_wait(barrier, plane - 1 + level * plane)
+
+    @pl.when(level > 0)
+    def _():
+        pl.semaphore_signal(ready, inc=1, device_id={"trade": me - plane}, device_id_type=MESH)
+
+    def send(j, src, out_sem, sem):
+        pltpu.make_async_remote_copy(
+            src_ref=src,
+            dst_ref=src,
+            send_sem=out_sem,
+            recv_sem=sem,
             device_id={"trade": j},
             device_id_type=MESH,
-        )
-
-    each_peer(lambda j: gather(j).start())
+        ).start()
+
+    own.wait()
+    each_near(lambda j: send(j, fact.at[me], gs_sem, near_sem))
+    each_of(0, level * plane, lambda j: send(j, fact.at[me], gs_sem, high_sem))
 
     for copy in copies:
         copy.wait()
@@ -146,7 +177,36 @@
             side = slice(h, h + LANES)
             coef_v[cut, side] = jnp.where(keep, coef_v[cut, side].astype(f32), 0.0).astype(bf16)
 
-    settle(fact, gr_sem)
+    def layer(i):
+        return fact.at[pl.ds(i * plane, plane)]
+
+    def settle_layer(sem):
+        pltpu.make_async_copy(layer(0), layer(0), sem).wait()
+
+    def relay(i):
+        @pl.when(inner)
+        def _():
+            send(me + plane, layer(i), up_sem, low_sem.at[i])
+
+    settle(fact, near_sem, plane - 1)
+
+    @pl.when(inner)
+    def _():
+        pl.semaphore_wait(ready, 1)
+
+    relay(level)
+
+    def climb(i):
+        settle_layer(low_sem.at[level - 1 - i])
+        relay(level - 1 - i)
+
+    each_of(0, level, climb)
+    for i in range(levels - 1):
+
+        @pl.when(level == i)
+        def _():
+            settle(fact, high_sem, (levels - 1 - i) * plane)
+
 
     for j in range(n):
         block = fact[j].astype(f32)
@@ -200,7 +260,7 @@
 
     each_peer(lambda j: scatter(j).start())
     recv[me] = part[me]
-    settle(recv, sr_sem)
+    settle(recv, sr_sem, n - 1)
 
     netted = recv[0]
     for j in range(1, n):
@@ -223,8 +283,15 @@
             own = jnp.where(lane_date == i, block, 0.0) if rep > 1 else block
             result = jnp.where(column == j * rep + i, jnp.sum(own, axis=1, keepdims=True), result)
     out[...] = result
-    settle(fact, gs_sem)
-    settle(recv, ss_sem)
+    for i in range(levels):
+
+        @pl.when(level == i)
+        def _():
+            settle(fact, gs_sem, plane - 1 + i * plane)
+            if i < levels - 1:
+                settle(fact, up_sem, (i + 1) * plane)
+
+    settle(recv, ss_sem, n - 1)
 
 
 def stay(x):
@@ -267,6 +334,10 @@
             pltpu.SemaphoreType.DMA,
             pltpu.SemaphoreType.DMA,
             pltpu.SemaphoreType.DMA,
+            pltpu.SemaphoreType.DMA((n // plane_size(n),)),
+            pltpu.SemaphoreType.REGULAR,
+            pltpu.SemaphoreType.DMA,
+            pltpu.SemaphoreType.DMA,
         ],
         compiler_params=pltpu.CompilerParams(
             collective_id=0, has_side_effects=True, vmem_limit_bytes=48 * 2**20

time: 17.3 us -> 20.6 us (1.19)
  Pallas kernels: 15.9 us -> 19.2 us
    pallas_call x1, Pallas kernels: 15.9 us -> 19.2 us  [body(): pl.pallas_call(functools.partial(kernel, n), out_shape=jax.ShapeDtypeStru...]
where the time goes in v5:
time: 20.6 us; the launch traced here: 20.5 us
  Pallas kernels  19.2 us (93%)
  between operations  0.66 us (3%)
  other arithmetic  0.56 us (3%)
    pallas_call x1, Pallas kernels, body(): pl.pallas_call(functools.partial(kernel, n), out_shape=jax.ShapeDtypeStru...  19.2 us
    div x1, other arithmetic, body(): return total / paths  0.56 us

profile of v5, /device:TPU:0, one launch (start us, length us, event | category | flops | bytes accessed | tf_op | source)
XLA Modules:
  0.0 20.5 jit_solution(6540283942727015533)
XLA Ops:
  0.7 19.2 %shard_map.91 = f32[2,8]{1,0:T(2,128)S(1)} custom-call(bf16[4,128]{1,0:T(4,128)(2,1)} %factors.1, f32[16,32]{1,0:T(8,128)} %bitcast.4, bf16[2048,256]{1,0:T(8,128)(2,1)} %trade_coef.1, s32[16,128]{1,0:T(8,128)} %bitcast.5, s32[1,2048]{1,0:T(1,128)} %bitcast.6, s32[1]{0:T(128)S(6)} %copy.10.live_count, s32[1,32]{1,0:T(1,128)} %bitcast.7, f32[2]{0:T(128)} %threshold.1, ...), custom_call_target="tpu_custom_call" | custom-call | tf_op jit(solution)/shard_map/pallas_call | solution.py:310
  19.9 0.6 %broadcast_multiply_fusion = f32[2,8]{1,0:T(2,128)} fusion(f32[2,8]{1,0:T(2,128)S(1)} %shard_map.91), kind=kLoop, calls=%fused_computation | loop fusion | flops 16 | bytes 128 | tf_op jit(solution)/shard_map/div | solution.py:356

commit v6 on v4

--- a/solution.py
+++ b/solution.py
@@ -66,11 +66,16 @@
     owned = recv.shape[1]
     sets = n * owned
 
-    def peer(k):
-        return lax.rem(me + k, n)
-
-    def each_peer(step):
-        lax.fori_loop(1, n, lambda k, c: (step(peer(k)), c)[1], 0)
+    def each_peer(step, last_first=False):
+        def at(i):
+            i = n - 2 - i if last_first else i
+            step(jnp.where(i >= me, i + 1, i))
+
+        if n <= LANES // 4:
+            for i in range(n - 1):
+                at(i)
+        else:
+            lax.fori_loop(0, n - 1, lambda i, c: (at(i), c)[1], 0)
 
     def local(src, dst, i):
         return pltpu.make_async_copy(src, dst, in_sem.at[i])
@@ -108,7 +113,7 @@
             device_id_type=MESH,
         )
 
-    each_peer(lambda j: gather(j).start())
+    each_peer(lambda j: gather(j).start(), last_first=True)
 
     for copy in copies:
         copy.wait()

time: 17.3 us -> 17.1 us (0.988)
  no operation moved by 1% of the time
where the time goes in v6:
time: 17.1 us; the launch traced here: 17 us
  Pallas kernels  15.8 us (92%)
  between operations  0.66 us (4%)
  other arithmetic  0.56 us (3%)
    pallas_call x1, Pallas kernels, body(): pl.pallas_call(functools.partial(kernel, n), out_shape=jax.ShapeDtypeStru...  15.8 us
    div x1, other arithmetic, body(): return total / paths  0.56 us

profile of v6, /device:TPU:0, one launch (start us, length us, event | category | flops | bytes accessed | tf_op | source)
XLA Modules:
  0.0 17.0 jit_solution(8858836814045606302)
XLA Ops:
  0.7 15.8 %shard_map.91 = f32[2,8]{1,0:T(2,128)S(1)} custom-call(bf16[4,128]{1,0:T(4,128)(2,1)} %factors.1, f32[16,32]{1,0:T(8,128)} %bitcast.4, bf16[2048,256]{1,0:T(8,128)(2,1)} %trade_coef.1, s32[16,128]{1,0:T(8,128)} %bitcast.5, s32[1,2048]{1,0:T(1,128)} %bitcast.6, s32[1]{0:T(128)S(6)} %copy.10.live_count, s32[1,32]{1,0:T(1,128)} %bitcast.7, f32[2]{0:T(128)} %threshold.1, ...), custom_call_target="tpu_custom_call" | custom-call | tf_op jit(solution)/shard_map/pallas_call | solution.py:248
  16.4 0.6 %broadcast_multiply_fusion = f32[2,8]{1,0:T(2,128)} fusion(f32[2,8]{1,0:T(2,128)S(1)} %shard_map.91), kind=kLoop, calls=%fused_computation | loop fusion | flops 16 | bytes 128 | tf_op jit(solution)/shard_map/div | solution.py:290

commit v7 on v6

--- a/solution.py
+++ b/solution.py
@@ -59,11 +59,13 @@
 ):
     me = lax.axis_index("trade")
     rows = fact.shape[1]
-    paths = n * rows
+    near = n // 2
+    paths = near * rows
     rep = max(1, LANES // paths)
     width = rep * paths
     slots = coef_v.shape[0]
-    owned = recv.shape[1]
+    owned = recv.shape[2]
+    mine = lax.div(me, near)
     sets = n * owned
 
     def each_peer(step, last_first=False):
@@ -80,8 +82,8 @@
     def local(src, dst, i):
         return pltpu.make_async_copy(src, dst, in_sem.at[i])
 
-    def settle(ref, sem):
-        rest = ref.at[pl.ds(0, n - 1)]
+    def settle(ref, sem, count):
+        rest = ref.at[pl.ds(0, count)]
         pltpu.make_async_copy(rest, rest, sem).wait()
 
     barrier = pltpu.get_barrier_semaphore()
@@ -108,7 +110,7 @@
             src_ref=fact.at[me],
             dst_ref=fact.at[me],
             send_sem=gs_sem,
-            recv_sem=gr_sem,
+            recv_sem=gr_sem.at[mine],
             device_id={"trade": j},
             device_id_type=MESH,
         )
@@ -136,8 +138,9 @@
         cut = slice(c * CHUNK, (c + 1) * CHUNK)
         onehot[:, cut] = (ids_v[:, cut] == owner_set).astype(f32).astype(bf16)
 
-    for i in range(LAG):
-        held[:, i * paths : (i + 1) * paths] = marg_v[...]
+    for half in range(2):
+        for i in range(LAG):
+            held[half, :, i * paths : (i + 1) * paths] = marg_v[:, half * paths : (half + 1) * paths]
 
     live_now = live_count[0]
     slot_index = iota(size_v.shape, 0) * LANES + iota(size_v.shape, 1)
@@ -151,85 +154,93 @@
             side = slice(h, h + LANES)
             coef_v[cut, side] = jnp.where(keep, coef_v[cut, side].astype(f32), 0.0).astype(bf16)
 
-    settle(fact, gr_sem)
-
-    for j in range(n):
-        block = fact[j].astype(f32)
-        for i in range(rep):
-            at = i * paths + j * rows
-            spread[at : at + rows] = block
-    table = spread[...].astype(bf16)
-    dims = (((1,), (1,)), ((), ()))
-    loaded = lax.dot_general(split[2], table, dims, preferred_element_type=f32)
-    loaded += lax.dot_general(split[1], table, dims, preferred_element_type=f32)
-    loaded += lax.dot_general(split[0], table, dims, preferred_element_type=f32)
-    bent = jnp.tanh(loaded)
-    tall = rep * K
-    pair = iota((tall, width), 0) // K == iota((tall, width), 1) // paths
-    for j in range(DATES // rep):
-        strip = jnp.where(pair, bent[j * tall : (j + 1) * tall], 0.0).astype(bf16)
-        basis[j * tall : (j + 1) * tall, j * width : (j + 1) * width] = strip
-
-    def block_sums(right):
-        total = None
-        for c in range(slots // CHUNK):
-            cut = slice(c * CHUNK, (c + 1) * CHUNK)
-            values = jnp.dot(coef_v[cut], right, preferred_element_type=f32).astype(bf16)
-            term = jnp.dot(onehot[:, cut], values, preferred_element_type=f32)
-            total = term if total is None else total + term
-        return total
-
-    blocks = acc.shape[1] // COLS
-    if blocks == 1:
-        acc[...] = block_sums(basis[...])
-    else:
-
-        def one(b, carry):
-            side = pl.ds(pl.multiple_of(b * COLS, COLS), COLS)
-            acc[:, side] = block_sums(basis[:, side])
-            return carry
-
-        lax.fori_loop(0, blocks, one, 0)
-    for j in range(n):
-        part[j] = acc[j * owned : (j + 1) * owned]
-
-    def scatter(j):
+    def half_sums(half):
+        for j in range(near):
+            block = fact[half * near + j].astype(f32)
+            for i in range(rep):
+                at = i * paths + j * rows
+                spread[at : at + rows] = block
+        table = spread[...].astype(bf16)
+        dims = (((1,), (1,)), ((), ()))
+        loaded = lax.dot_general(split[2], table, dims, preferred_element_type=f32)
+        loaded += lax.dot_general(split[1], table, dims, preferred_element_type=f32)
+        loaded += lax.dot_general(split[0], table, dims, preferred_element_type=f32)
+        bent = jnp.tanh(loaded)
+        tall = rep * K
+        pair = iota((tall, width), 0) // K == iota((tall, width), 1) // paths
+        for j in range(DATES // rep):
+            strip = jnp.where(pair, bent[j * tall : (j + 1) * tall], 0.0).astype(bf16)
+            basis[j * tall : (j + 1) * tall, j * width : (j + 1) * width] = strip
+
+        def block_sums(right):
+            total = None
+            for c in range(slots // CHUNK):
+                cut = slice(c * CHUNK, (c + 1) * CHUNK)
+                values = jnp.dot(coef_v[cut], right, preferred_element_type=f32).astype(bf16)
+                term = jnp.dot(onehot[:, cut], values, preferred_element_type=f32)
+                total = term if total is None else total + term
+            return total
+
+        blocks = max(1, acc.shape[1] // COLS)
+        if blocks == 1:
+            acc[...] = block_sums(basis[...])
+        else:
+
+            def one(b, carry):
+                side = pl.ds(pl.multiple_of(b * COLS, COLS), COLS)
+                acc[:, side] = block_sums(basis[:, side])
+                return carry
+
+            lax.fori_loop(0, blocks, one, 0)
+        for j in range(n):
+            part[half, j] = acc[j * owned : (j + 1) * owned]
+
+    def scatter(j, half, stage):
         return pltpu.make_async_remote_copy(
-            src_ref=part.at[j],
-            dst_ref=recv.at[me],
-            send_sem=ss_sem,
-            recv_sem=sr_sem,
+            src_ref=part.at[half, j],
+            dst_ref=recv.at[half, me],
+            send_sem=ss_sem.at[stage],
+            recv_sem=sr_sem.at[half],
             device_id={"trade": j},
             device_id_type=MESH,
         )
 
-    each_peer(lambda j: scatter(j).start())
-    recv[me] = part[me]
-    settle(recv, sr_sem)
-
-    netted = recv[0]
-    for j in range(1, n):
-        netted = netted + recv[j]
+    settle(fact, gr_sem.at[mine], near - 1)
+    half_sums(mine)
+    each_peer(lambda j: scatter(j, mine, 0).start())
+    settle(fact, gr_sem.at[1 - mine], near)
+    half_sums(1 - mine)
+    each_peer(lambda j: scatter(j, 1 - mine, 1).start())
+    for half in range(2):
+        recv[half, me] = part[half, me]
+    settle(recv.at[0], sr_sem.at[0], n - 1)
+    settle(recv.at[1], sr_sem.at[1], n - 1)
+
     row_at = iota((owned, 1), 0)
     limits = jnp.zeros((owned, 1), f32)
     for r in range(owned):
         limits = jnp.where(row_at == r, thr_s[r], limits)
     first = LAG * paths
-    margin = jnp.maximum(netted[:, : (DATES - LAG) * paths] - limits, 0.0)
-    head = jnp.maximum(netted[:, :first] - held[...], 0.0)
-    tail = jnp.maximum(netted[:, first:] - margin, 0.0)
     result = jnp.zeros(out.shape, f32)
     lane_date = iota((owned, width), 1) // paths
     column = iota(out.shape, 1)
+    short = jnp.zeros((owned, DATES * paths), f32)
+    for half in range(2):
+        netted = recv[half, 0]
+        for j in range(1, n):
+            netted = netted + recv[half, j]
+        margin = jnp.maximum(netted[:, : (DATES - LAG) * paths] - limits, 0.0)
+        collateral = jnp.concatenate([held[half], margin], axis=1)
+        short = short + jnp.maximum(netted - collateral, 0.0)
     for j in range(DATES // rep):
-        at = j * width
-        block = head[:, at : at + width] if at < first else tail[:, at - first : at - first + width]
+        block = short[:, j * width : (j + 1) * width]
         for i in range(rep):
-            own = jnp.where(lane_date == i, block, 0.0) if rep > 1 else block
-            result = jnp.where(column == j * rep + i, jnp.sum(own, axis=1, keepdims=True), result)
+            own_date = jnp.where(lane_date == i, block, 0.0) if rep > 1 else block
+            result = jnp.where(column == j * rep + i, jnp.sum(own_date, axis=1, keepdims=True), result)
     out[...] = result
-    settle(fact, gs_sem)
-    settle(recv, ss_sem)
+    settle(fact, gs_sem, n - 1)
+    settle(recv.at[0], ss_sem.at[0], n - 1)
+    settle(recv.at[1], ss_sem.at[1], n - 1)
 
 
 def stay(x):
@@ -239,11 +250,12 @@
 def body(n, factors, loadings, trade_coef, basis_size, set_ids, live_count, netting_row, threshold, margin_start):
     rows = factors.shape[0]
     paths = n * rows
-    rep = max(1, LANES // paths)
+    half = paths // 2
+    rep = max(1, LANES // half)
     slots = trade_coef.shape[0]
     sets = netting_row.shape[0]
     owned = threshold.shape[0]
-    wide = DATES * paths
+    wide = DATES * half
     hbm = pl.BlockSpec(memory_space=pltpu.MemorySpace.HBM)
     total = pl.pallas_call(
         functools.partial(kernel, n),
@@ -261,17 +273,17 @@
             pltpu.VMEM((owned, paths), f32),
             pltpu.VMEM((3, DATES * K, DATES * F), bf16),
             pltpu.VMEM((sets, slots), bf16),
-            pltpu.VMEM((rep * paths, DATES * F), f32),
+            pltpu.VMEM((rep * half, DATES * F), f32),
             pltpu.VMEM((DATES * K, wide), bf16),
-            pltpu.VMEM((owned, LAG * paths), f32),
+            pltpu.VMEM((2, owned, LAG * half), f32),
             pltpu.VMEM((sets, wide), f32),
-            pltpu.VMEM((n, owned, wide), f32),
-            pltpu.VMEM((n, owned, wide), f32),
+            pltpu.VMEM((2, n, owned, wide), f32),
+            pltpu.VMEM((2, n, owned, wide), f32),
             pltpu.SemaphoreType.DMA((3,)),
             pltpu.SemaphoreType.DMA,
-            pltpu.SemaphoreType.DMA,
-            pltpu.SemaphoreType.DMA,
-            pltpu.SemaphoreType.DMA,
+            pltpu.SemaphoreType.DMA((2,)),
+            pltpu.SemaphoreType.DMA((2,)),
+            pltpu.SemaphoreType.DMA((2,)),
         ],
         compiler_params=pltpu.CompilerParams(
             collective_id=0, has_side_effects=True, vmem_limit_bytes=48 * 2**20

time: 17.1 us -> 16.6 us (0.971)
  Pallas kernels: 15.8 us -> 15.3 us
    pallas_call x1, Pallas kernels: 15.8 us -> 15.3 us  [body(): pl.pallas_call(functools.partial(kernel, n), out_shape=jax.ShapeDtypeStru...]
where the time goes in v7:
time: 16.6 us; the launch traced here: 16.5 us
  Pallas kernels  15.3 us (92%)
  between operations  0.66 us (4%)
  other arithmetic  0.56 us (3%)
    pallas_call x1, Pallas kernels, body(): pl.pallas_call(functools.partial(kernel, n), out_shape=jax.ShapeDtypeStru...  15.3 us
    div x1, other arithmetic, body(): return total / paths  0.56 us

profile of v7, /device:TPU:0, one launch (start us, length us, event | category | flops | bytes accessed | tf_op | source)
XLA Modules:
  0.0 16.5 jit_solution(17986282571291424721)
XLA Ops:
  0.7 15.3 %shard_map.91 = f32[2,8]{1,0:T(2,128)S(1)} custom-call(bf16[4,128]{1,0:T(4,128)(2,1)} %factors.1, f32[16,32]{1,0:T(8,128)} %bitcast.4, bf16[2048,256]{1,0:T(8,128)(2,1)} %trade_coef.1, s32[16,128]{1,0:T(8,128)} %bitcast.5, s32[1,2048]{1,0:T(1,128)} %bitcast.6, s32[1]{0:T(128)S(6)} %copy.10.live_count, s32[1,32]{1,0:T(1,128)} %bitcast.7, f32[2]{0:T(128)} %threshold.1, ...), custom_call_target="tpu_custom_call" | custom-call | tf_op jit(solution)/shard_map/pallas_call | solution.py:260
  15.9 0.6 %broadcast_multiply_fusion = f32[2,8]{1,0:T(2,128)} fusion(f32[2,8]{1,0:T(2,128)S(1)} %shard_map.91), kind=kLoop, calls=%fused_computation | loop fusion | flops 16 | bytes 128 | tf_op jit(solution)/shard_map/div | solution.py:302
